TPU v7x, 32 devices: a whole 2x2x4 slice. The times are simulated.
32 devices in a mesh: fsdp: 4 (over y, x), seq: 8 (over z, core).
Axes of the slice: x: 2, y: 2, z: 4, core: 2. Of those that a mesh axis runs over, the one named last changes fastest.
Arguments:
- residual_in: bfloat16 [4, 1024, 2048], P('fsdp', 'seq'), may hold values from -6 to 6
- attn_gain: bfloat16 [2048], replicated, may hold values from 0.5 to 1.5
- mlp_gain: bfloat16 [2048], replicated, may hold values from 0.5 to 1.5
- w_qkv: bfloat16 [2048, 3, 2048], P('fsdp'), may hold values from -0.125 to 0.125
- w_out: bfloat16 [2048, 2048], P('fsdp'), may hold values from -1 to 1
- w_gate_up: bfloat16 [8192, 2, 2048], P('fsdp'), may hold values from -0.125 to 0.125
- w_down: bfloat16 [2048, 8192], P('fsdp'), may hold values from -0.0625 to 0.0625
- cotangent: bfloat16 [4, 1024, 2048], P('fsdp', 'seq'), may hold values from -6 to 6
Outputs:
- layer_out: bfloat16 [4, 1024, 2048], P('fsdp', 'seq')
- grad_input: float32 [4, 1024, 2048], P('fsdp', 'seq')
- grad_attn_gain: float32 [2048], P(('fsdp', 'seq'))
- grad_mlp_gain: float32 [2048], P(('fsdp', 'seq'))
- grad_qkv: float32 [2048, 3, 2048], P(('seq', 'fsdp'))
- grad_out_proj: float32 [2048, 2048], P(None, ('seq', 'fsdp'))
- grad_gate_up: float32 [8192, 2, 2048], P(('seq', 'fsdp'))
- grad_down: float32 [2048, 8192], P(None, ('seq', 'fsdp'))
All inputs are finite; a program needn't handle non-finite values.
Results may differ from a plain program's by a relative error of at most 0.018.
Values may be sent and summed in bfloat16 or wider, within the bound.
No kernel may reach another device: no remote copies, remote signals or barrier semaphores. Data moves between devices by JAX's collectives and lax.ppermute only.
A program may use at most 384 MiB of HBM per device.

v0:
```python
import math
import jax
import jax.numpy as jnp
from jax import lax
from jax.sharding import PartitionSpec as P

HD = 64
NORM_EPS = 1e-05
ROPE_BASE = 130000.0


def rotate(matrix):
    shaped = matrix.reshape(matrix.shape[:-1] + (matrix.shape[-1] // HD, 2, HD // 2))
    turned = jnp.stack([-shaped[..., 1, :], shaped[..., 0, :]], axis=-2)
    return turned.reshape(matrix.shape)


def rotate_back(matrix):
    shaped = matrix.reshape(matrix.shape[:-1] + (matrix.shape[-1] // HD, 2, HD // 2))
    turned = jnp.stack([shaped[..., 1, :], -shaped[..., 0, :]], axis=-2)
    return turned.reshape(matrix.shape)


def rope_tables(positions, columns):
    freq_index = (jnp.arange(columns, dtype=jnp.int32) % (HD // 2)).astype(jnp.float32)
    inverse = ROPE_BASE ** (-2.0 * freq_index / HD)
    angles = positions.astype(jnp.float32)[:, None] * inverse[None, :]
    return (jnp.cos(angles), jnp.sin(angles))


def rms_scale(matrix):
    return lax.rsqrt(jnp.mean(matrix * matrix, axis=-1, keepdims=True) + NORM_EPS)


def rms_back(grad_normed, matrix, scale_rows, gain):
    weighted = grad_normed * gain
    inner_mean = jnp.mean(weighted * matrix, axis=-1, keepdims=True)
    grad_matrix = scale_rows * weighted - matrix * scale_rows**3 * inner_mean
    grad_gain = jnp.sum(grad_normed * matrix * scale_rows, axis=0)
    return (grad_matrix, grad_gain)


def attend_forward(queries, key_rows, values):
    seq_count, length, width_here = queries.shape
    heads_here = width_here // HD
    q_block = min(512, length)
    k_block = min(256, length)
    inv_root = 1.0 / math.sqrt(HD)
    shaped_q = queries.reshape(seq_count, length, heads_here, HD)
    shaped_k = key_rows.reshape(seq_count, length, heads_here, HD)
    shaped_v = values.reshape(seq_count, length, heads_here, HD)

    def query_step(q_index, carried):
        attended, totals = carried
        offset = q_index * q_block
        q_rows = lax.dynamic_slice_in_dim(shaped_q, offset, q_block, 1)
        query_pos = offset + jnp.arange(q_block, dtype=jnp.int32)

        def key_step(k_index, running):
            unnorm, denominator = running
            k_start = k_index * k_block
            k_rows = lax.dynamic_slice_in_dim(shaped_k, k_start, k_block, 1)
            v_rows = lax.dynamic_slice_in_dim(shaped_v, k_start, k_block, 1)
            scores = (
                jnp.einsum("bqhd,bkhd->bhqk", q_rows, k_rows, preferred_element_type=jnp.float32)
                * inv_root
            )
            causal = (k_start + jnp.arange(k_block, dtype=jnp.int32))[None, :] <= query_pos[:, None]
            exp_scores = jnp.where(causal, jnp.exp(scores), 0.0)
            denominator = denominator + jnp.sum(exp_scores, axis=-1)
            unnorm = unnorm + jnp.einsum(
                "bhqk,bkhd->bqhd",
                exp_scores.astype(jnp.bfloat16),
                v_rows,
                preferred_element_type=jnp.float32,
            )
            return (unnorm, denominator)

        start_state = (
            jnp.zeros((seq_count, q_block, heads_here, HD), jnp.float32),
            jnp.zeros((seq_count, heads_here, q_block), jnp.float32),
        )
        unnorm, denominator = lax.fori_loop(0, (offset + q_block) // k_block, key_step, start_state)
        block_out = unnorm / jnp.transpose(denominator, (0, 2, 1))[..., None]
        attended = lax.dynamic_update_slice_in_dim(attended, block_out, offset, 1)
        totals = lax.dynamic_update_slice_in_dim(totals, denominator, offset, 2)
        return (attended, totals)

    initial = (
        jnp.zeros((seq_count, length, heads_here, HD), jnp.float32),
        jnp.zeros((seq_count, heads_here, length), jnp.float32),
    )
    attended, totals = lax.fori_loop(0, length // q_block, query_step, initial)
    return (attended.reshape(seq_count, length, width_here), totals)


def attend_backward(queries, key_rows, values, attended, totals, grad_attended):
    seq_count, length, width_here = queries.shape
    heads_here = width_here // HD
    q_block = min(512, length)
    k_block = min(256, length)
    inv_root = 1.0 / math.sqrt(HD)
    shaped_q = queries.reshape(seq_count, length, heads_here, HD)
    shaped_k = key_rows.reshape(seq_count, length, heads_here, HD)
    shaped_v = values.reshape(seq_count, length, heads_here, HD)
    shaped_grad = grad_attended.reshape(seq_count, length, heads_here, HD).astype(jnp.float32)
    shaped_att = attended.reshape(seq_count, length, heads_here, HD)
    totals_rows = jnp.transpose(totals, (0, 2, 1))
    grad_total = -jnp.sum(shaped_grad * shaped_att, axis=-1) / totals_rows
    grad_unnorm = (shaped_grad / totals_rows[..., None]).astype(jnp.bfloat16)

    def query_step(q_index, carried):
        grad_q, grad_k, grad_v = carried
        offset = q_index * q_block
        q_rows = lax.dynamic_slice_in_dim(shaped_q, offset, q_block, 1)
        g_rows = lax.dynamic_slice_in_dim(grad_unnorm, offset, q_block, 1)
        total_rows = jnp.transpose(
            lax.dynamic_slice_in_dim(grad_total, offset, q_block, 1), (0, 2, 1)
        )
        query_pos = offset + jnp.arange(q_block, dtype=jnp.int32)

        def key_step(k_index, running):
            dq_acc, dk_all, dv_all = running
            k_start = k_index * k_block
            k_rows = lax.dynamic_slice_in_dim(shaped_k, k_start, k_block, 1)
            v_rows = lax.dynamic_slice_in_dim(shaped_v, k_start, k_block, 1)
            scores = (
                jnp.einsum("bqhd,bkhd->bhqk", q_rows, k_rows, preferred_element_type=jnp.float32)
                * inv_root
            )
            causal = (k_start + jnp.arange(k_block, dtype=jnp.int32))[None, :] <= query_pos[:, None]
            exp_scores = jnp.where(causal, jnp.exp(scores), 0.0)
            grad_prob = jnp.einsum(
                "bqhd,bkhd->bhqk", g_rows, v_rows, preferred_element_type=jnp.float32
            )
            grad_scores = (exp_scores * (grad_prob + total_rows[..., None])).astype(jnp.bfloat16)
            dq_acc = (
                dq_acc
                + jnp.einsum(
                    "bhqk,bkhd->bqhd", grad_scores, k_rows, preferred_element_type=jnp.float32
                )
                * inv_root
            )
            dk_part = (
                jnp.einsum(
                    "bhqk,bqhd->bkhd", grad_scores, q_rows, preferred_element_type=jnp.float32
                )
                * inv_root
            )
            dv_part = jnp.einsum(
                "bhqk,bqhd->bkhd",
                exp_scores.astype(jnp.bfloat16),
                g_rows,
                preferred_element_type=jnp.float32,
            )
            dk_slice = lax.dynamic_slice_in_dim(dk_all, k_start, k_block, 1) + dk_part
            dv_slice = lax.dynamic_slice_in_dim(dv_all, k_start, k_block, 1) + dv_part
            dk_all = lax.dynamic_update_slice_in_dim(dk_all, dk_slice, k_start, 1)
            dv_all = lax.dynamic_update_slice_in_dim(dv_all, dv_slice, k_start, 1)
            return (dq_acc, dk_all, dv_all)

        start_state = (jnp.zeros((seq_count, q_block, heads_here, HD), jnp.float32), grad_k, grad_v)
        dq_block, grad_k, grad_v = lax.fori_loop(
            0, (offset + q_block) // k_block, key_step, start_state
        )
        grad_q = lax.dynamic_update_slice_in_dim(grad_q, dq_block, offset, 1)
        return (grad_q, grad_k, grad_v)

    empty = jnp.zeros((seq_count, length, heads_here, HD), jnp.float32)
    grad_q, grad_k, grad_v = lax.fori_loop(0, length // q_block, query_step, (empty, empty, empty))
    cosine, sine_table = rope_tables(jnp.arange(length, dtype=jnp.int32), width_here)
    grad_q = grad_q.reshape(seq_count, length, width_here)
    grad_k = grad_k.reshape(seq_count, length, width_here)
    grad_v = grad_v.reshape(seq_count, length, width_here)
    raw_q = grad_q * cosine + rotate_back(grad_q * sine_table)
    raw_k = grad_k * cosine + rotate_back(grad_k * sine_table)
    return jnp.stack([raw_q, raw_k, grad_v]).astype(jnp.bfloat16)


def body(residual_in, attn_gain, mlp_gain, w_qkv, w_out, w_gate_up, w_down, cotangent):
    seq_count, shard_len, model_width = residual_in.shape
    tokens = seq_count * shard_len
    seq_index = lax.axis_index("seq")
    positions = seq_index * shard_len + jnp.arange(tokens, dtype=jnp.int32) % shard_len
    cosine, sine_table = rope_tables(positions, model_width)
    inputs = residual_in.reshape(tokens, model_width).astype(jnp.float32)
    gain_one = attn_gain.astype(jnp.float32)
    gain_two = mlp_gain.astype(jnp.float32)
    scale_one = rms_scale(inputs)
    normed_one = (inputs * scale_one * gain_one).astype(jnp.bfloat16)
    qkv_full, out_full = (
        lax.all_gather(w_qkv, "fsdp", axis=0, tiled=True),
        lax.all_gather(w_out, "fsdp", axis=0, tiled=True),
    )
    projected = jnp.einsum("td,fpd->ptf", normed_one, qkv_full, preferred_element_type=jnp.float32)
    queries = (projected[0] * cosine + rotate(projected[0]) * sine_table).astype(jnp.bfloat16)
    key_rows = (projected[1] * cosine + rotate(projected[1]) * sine_table).astype(jnp.bfloat16)
    values = projected[2].astype(jnp.bfloat16)
    stacked = jnp.stack([queries, key_rows, values]).reshape(3, seq_count, shard_len, model_width)
    head_view = lax.all_to_all(stacked, "seq", split_axis=3, concat_axis=2, tiled=True)
    attended, totals = attend_forward(head_view[0], head_view[1], head_view[2])
    attended_heads = attended.astype(jnp.bfloat16)
    sent_back = lax.all_to_all(attended_heads, "seq", split_axis=1, concat_axis=2, tiled=True)
    attended_low = sent_back.reshape(tokens, model_width)
    branch = jnp.einsum("ti,fi->tf", attended_low, out_full, preferred_element_type=jnp.float32)
    residual = inputs + branch
    scale_two = rms_scale(residual)
    normed_two = (residual * scale_two * gain_two).astype(jnp.bfloat16)
    up_full, down_full = (
        lax.all_gather(w_gate_up, "fsdp", axis=0, tiled=True),
        lax.all_gather(w_down, "fsdp", axis=0, tiled=True),
    )
    gate_up = jnp.einsum("td,jpd->ptj", normed_two, up_full, preferred_element_type=jnp.float32)
    hidden = (jax.nn.silu(gate_up[0]) * gate_up[1]).astype(jnp.bfloat16)
    mlp_term = jnp.einsum("tj,fj->tf", hidden, down_full, preferred_element_type=jnp.float32)
    layer_out = (
        (residual + mlp_term).astype(jnp.bfloat16).reshape(seq_count, shard_len, model_width)
    )
    grad_out = cotangent.reshape(tokens, model_width)
    up_again, down_again = (
        lax.all_gather(w_gate_up, "fsdp", axis=0, tiled=True),
        lax.all_gather(w_down, "fsdp", axis=0, tiled=True),
    )
    grad_hidden = jnp.einsum("tf,fj->tj", grad_out, down_again, preferred_element_type=jnp.float32)
    sigmoid_gate = jax.nn.sigmoid(gate_up[0])
    grad_gate = grad_hidden * gate_up[1] * sigmoid_gate * (1.0 + gate_up[0] * (1.0 - sigmoid_gate))
    grad_up = grad_hidden * jax.nn.silu(gate_up[0])
    grad_gu = jnp.stack([grad_gate, grad_up]).astype(jnp.bfloat16)
    grad_normed_two = jnp.einsum(
        "ptj,jpd->td", grad_gu, up_again, preferred_element_type=jnp.float32
    )
    ff_width = grad_gu.shape[2]
    unit_rows = jnp.concatenate([grad_gu, hidden[None]], axis=0).reshape(
        3, seq_count, shard_len, ff_width
    )
    unit_cols = lax.all_to_all(unit_rows, "seq", split_axis=3, concat_axis=2, tiled=True)
    normed_piece = lax.all_gather(
        normed_two.reshape(seq_count, shard_len, model_width), "seq", axis=1, tiled=True
    )
    grad_piece = lax.all_gather(cotangent, "seq", axis=1, tiled=True)
    gu_part = jnp.einsum(
        "psnj,snd->jpd", unit_cols[:2], normed_piece, preferred_element_type=jnp.float32
    )
    down_part = jnp.einsum(
        "snf,snj->fj", grad_piece, unit_cols[2], preferred_element_type=jnp.float32
    )
    gu_part, down_part = (gu_part, down_part)
    grad_gate_up, grad_down = (
        lax.psum_scatter(
            gu_part.astype(jnp.bfloat16), "fsdp", scatter_dimension=0, tiled=True
        ).astype(jnp.float32),
        lax.psum_scatter(
            down_part.astype(jnp.bfloat16), "fsdp", scatter_dimension=1, tiled=True
        ).astype(jnp.float32),
    )
    grad_norm_two, grad_gain_two = rms_back(grad_normed_two, residual, scale_two, gain_two)
    grad_residual = grad_out.astype(jnp.float32) + grad_norm_two
    qkv_back, out_back = (
        lax.all_gather(w_qkv, "fsdp", axis=0, tiled=True),
        lax.all_gather(w_out, "fsdp", axis=0, tiled=True),
    )
    grad_branch = grad_residual.astype(jnp.bfloat16)
    grad_attended = jnp.einsum(
        "tf,fi->ti", grad_branch, out_back, preferred_element_type=jnp.float32
    )
    grad_attended = grad_attended.astype(jnp.bfloat16).reshape(seq_count, shard_len, model_width)
    grad_heads = lax.all_to_all(grad_attended, "seq", split_axis=2, concat_axis=1, tiled=True)
    grad_stacked = attend_backward(
        head_view[0], head_view[1], head_view[2], attended, totals, grad_heads
    )
    normed_piece = lax.all_gather(
        normed_one.reshape(seq_count, shard_len, model_width), "seq", axis=1, tiled=True
    )
    branch_piece = lax.all_gather(
        grad_branch.reshape(seq_count, shard_len, model_width), "seq", axis=1, tiled=True
    )
    grad_piece = grad_stacked
    qkv_part = jnp.einsum(
        "psnf,snd->fpd", grad_piece, normed_piece, preferred_element_type=jnp.float32
    )
    out_part = jnp.einsum(
        "snf,sni->fi", branch_piece, attended_heads, preferred_element_type=jnp.float32
    )
    qkv_part, out_part = (qkv_part, out_part)
    grad_qkv, grad_out_proj = (
        lax.psum_scatter(
            qkv_part.astype(jnp.bfloat16), "fsdp", scatter_dimension=0, tiled=True
        ).astype(jnp.float32),
        lax.psum_scatter(
            out_part.astype(jnp.bfloat16), "fsdp", scatter_dimension=1, tiled=True
        ).astype(jnp.float32),
    )
    grad_projected = lax.all_to_all(grad_stacked, "seq", split_axis=2, concat_axis=3, tiled=True)
    grad_projected = grad_projected.reshape(3, tokens, model_width)
    grad_normed_one = jnp.einsum(
        "ptf,fpd->td", grad_projected, qkv_back, preferred_element_type=jnp.float32
    )
    grad_norm_one, grad_gain_one = rms_back(grad_normed_one, inputs, scale_one, gain_one)
    grad_input = (grad_residual + grad_norm_one).reshape(seq_count, shard_len, model_width)
    grad_attn_gain, grad_mlp_gain = (
        lax.psum_scatter(grad_gain_one, ("fsdp", "seq"), scatter_dimension=0, tiled=True),
        lax.psum_scatter(grad_gain_two, ("fsdp", "seq"), scatter_dimension=0, tiled=True),
    )
    return (
        layer_out,
        grad_input,
        grad_attn_gain,
        grad_mlp_gain,
        grad_qkv,
        grad_out_proj,
        grad_gate_up,
        grad_down,
    )


def solution(mesh):
    return jax.shard_map(
        body,
        mesh=mesh,
        in_specs=(
            P("fsdp", "seq", None),
            P(),
            P(),
            P("fsdp", None, None),
            P("fsdp", None),
            P("fsdp", None, None),
            P("fsdp", None),
            P("fsdp", "seq", None),
        ),
        out_specs=(
            P("fsdp", "seq", None),
            P("fsdp", "seq", None),
            P(("fsdp", "seq")),
            P(("fsdp", "seq")),
            P(("seq", "fsdp"), None, None),
            P(None, ("seq", "fsdp")),
            P(("seq", "fsdp"), None, None),
            P(None, ("seq", "fsdp")),
        ),
        check_vma=False,
    )
```

profile of v0, /device:TPU:0, one launch (start us, length us, event | category | flops | bytes accessed | tf_op | source)
XLA Modules:
  0.0 1827.8 jit_solution(5378411040820716253)
XLA Ops:
  8.7 18.1 copy.202
  28.7 211.5 %all-gather.11.cloned.1.call-done = bf16[2048,3,2048]{2,0,1:T(8,128)(2,1)} async-done(((bf16[512,3,2048]{2,0,1:T(8,128)(2,1)}), bf16[2048,3,2048]{2,0,1:T(8,128)(2,1)}) %all-gather.11.cloned.1.call-update) | async-done | bytes 25165840 | tf_op jit(solution)/shard_map/all_gather | solution.py:192
  240.2 13.5 convolution_bitcast_fusion.3
  270.8 5.3 fusion.111
  278.9 5.1 all-to-all-start
  284.0 49.0 %all-to-all-done = bf16[3,1,128,2048]{2,0,1,3:T(4,128)(2,1)S(1)} async-done(((bf16[3,1,128,2048]{2,0,1,3:T(4,128)(2,1)}), bf16[3,1,128,2048]{2,0,1,3:T(4,128)(2,1)S(1)}, u32[]{:S(2)}, u32[]{:S(2)}) %all-to-all-start) | async-done | bytes 1572896 | tf_op jit(solution)/shard_map/all_to_all | solution.py:200
  340.4 17.2 while.118
  341.2 5.1 while.121
  347.3 10.2 while.121
  358.5 3.6 copy.200
  362.7 5.9 reduce.3
  370.7 4.1 all-to-all-start.1
  376.2 14.0 all-to-all-done.1
  395.3 6.5 multiply_reduce_fusion.3
  402.0 506.1 %all-gather.15.cloned.1.call-done = bf16[8192,2,2048]{2,0,1:T(8,128)(2,1)} async-done(((bf16[2048,2,2048]{2,0,1:T(8,128)(2,1)}), bf16[8192,2,2048]{2,0,1:T(8,128)(2,1)}) %all-gather.15.cloned.1.call-update) | async-done | bytes 67108880 | tf_op jit(solution)/shard_map/all_gather | solution.py:210
  908.1 37.6 %convolution_bitcast_fusion.2 = f32[2,128,8192]{2,1,0:T(8,128)} fusion(bf16[8192,2,2048]{2,0,1:T(8,128)(2,1)} %all-gather.15.cloned.1.call-done, bf16[128,2048]{1,0:T(8,128)(2,1)S(1)} %multiply_convert_fusion.2), kind=kOutput, calls=%fused_computation.67 | convolution fusion | flops 8589934592 | bytes 76021760 | tf_op jit(solution)/shard_map/td,jpd->ptj/dot_general | solution.py:213
  945.7 261.2 %all-gather.17.cloned.1.call-done = bf16[2048,8192]{1,0:T(8,128)(2,1)} async-done(((bf16[512,8192]{1,0:T(8,128)(2,1)}), bf16[2048,8192]{1,0:T(8,128)(2,1)}) %all-gather.17.cloned.1.call-update) | async-done | bytes 33554448 | tf_op jit(solution)/shard_map/all_gather | solution.py:211
  1206.9 19.1 %fusion.83 = (bf16[1,128,8192]{2,1,0:T(8,128)(2,1)}, bf16[1,128,8192]{2,1,0:T(8,128)(2,1)}) fusion(f32[2,128,8192]{2,1,0:T(8,128)} %convolution_bitcast_fusion.2, bf16[2048,8192]{1,0:T(8,128)(2,1)} %all-gather.17.cloned.1.call-done, bf16[1,128,2048]{2,1,0:T(8,128)(2,1)} %param.23), kind=kOutput, calls=%fused_computation.108 | convolution fusion | flops 4308598784 | bytes 46661632 | tf_op jit(solution)/shard_map/tf,fj->tj/dot_general | solution.py:224
  1226.0 25.3 %multiply_reduce_fusion = (f32[2048]{0:T(1024)}, f32[128]{0:T(128)S(1)}, f32[128,2048]{1,0:T(8,128)S(1)}) fusion(f32[128,2048]{1,0:T(8,128)S(1)} %get-tuple-element.716, f32[128]{0:T(128)S(1)} %get-tuple-element.714, f32[2048]{0:T(1024)S(1)} %convert_element_type.212, bf16[8192,2,2048]{2,0,1:T(8,128)(2,1)} %all-gather.15.cloned.1.call-done, ...), kind=kOutput, calls=%fused_computation.151 | convolution fusion | flops 8593602560 | bytes 73417728 | tf_op jit(solution)/shard_map/ptj,jpd->td/dot_general | solution.py:229
  1254.4 6.0 multiply_convert_fusion
  1260.3 4.9 fusion.79
  1266.0 11.5 reduce.4
  1278.4 4.5 all-to-all-start.2
  1282.9 6.5 maximum_bitcast_fusion
  1289.4 13.2 copy.216
  1302.6 8.8 all-to-all-done.2
  1311.3 4.9 all-to-all-start.4
  1329.4 37.3 %while.120 = (s32[]{:T(128)}, f32[1,1024,4,64]{1,3,2,0:T(8,128)}, f32[1,1024,4,64]{1,3,2,0:T(8,128)S(1)}, f32[1,1024,4,64]{1,3,2,0:T(8,128)}, bf16[1,1024,4,64]{...) while((s32[]{:T(128)}, f32[1,1024,4,64]{1,3,2,0:T(8,128)}, ...), condition=%wide.region_12.13_spmd, body=%wide.region_9.12_spmd.sunk | while | flops 340329248 | bytes 17070880 | solution.py:170
  1331.2 10.7 while.122
  1344.5 21.4 %while.122 = (s32[]{:T(128)}, f32[1,512,4,64]{1,3,2,0:T(8,128)S(1)}, f32[1,1024,4,64]{1,3,2,0:T(8,128)S(1)}, f32[1,1024,4,64]{1,3,2,0:T(8,128)}, s32[]{:T(128)},...) while((s32[]{:T(128)}, f32[1,512,4,64]{1,3,2,0:T(8,128)S(1)}, ...), condition=%wide.region_11.11_spmd.clone, body=%wide.region_10.10_spmd.clone.sunk | while | flops 340329216 | bytes 14432507 | solution.py:163
  1368.0 4.7 fusion.115
  1384.9 5.2 add_convert_fusion.1
  1390.2 7.5 fusion.72
  1397.7 7.8 copy.215
  1405.6 4.4 convolution_convert_fusion
  1410.0 157.5 %all-to-all-done.4 = bf16[3,1,128,8192]{2,0,1,3:T(4,128)(2,1)} async-done(((bf16[3,1,128,8192]{2,0,1,3:T(4,128)(2,1)}), bf16[3,1,128,8192]{2,0,1,3:T(4,128)(2,1)}, u32[]{:S(2)}, u32[]{:S(2)}) %all-to-all-start.4) | async-done | bytes 6291488 | tf_op jit(solution)/shard_map/all_to_all | solution.py:236
  1567.5 4.6 copy.217
  1577.6 9.5 convert_bitcast_fusion.1
  1587.1 4.6 slice.103
  1591.7 6.3 copy.218
  1598.0 14.1 convert_bitcast_fusion
  1616.2 3.8 all-to-all-start.3
  1621.3 19.0 %fusion.80 = bf16[1,128,2048]{2,1,0:T(8,128)(2,1)} fusion(f32[128,2048]{1,0:T(8,128)S(1)} %copy-done.5, bf16[2048,8192]{1,0:T(8,128)(2,1)} %all-gather.17.cloned.1.call-done, f32[2,128,8192]{2,1,0:T(8,128)} %convolution_bitcast_fusion.2), kind=kOutput, calls=%fused_computation.106 | convolution fusion | flops 4301783040 | bytes 43515904 | tf_op jit(solution)/shard_map/tj,fj->tf/dot_general | solution.py:215
  1640.2 28.7 %all-to-all-done.3 = bf16[3,1,1024,256]{3,0,1,2:T(4,128)(2,1)S(1)} async-done(((bf16[3,1,1024,256]{3,0,1,2:T(4,128)(2,1)}), bf16[3,1,1024,256]{3,0,1,2:T(4,128)(2,1)S(1)}, u32[]{:S(2)}, u32[]{:S(2)}) %all-to-all-start.3) | async-done | bytes 1572896 | tf_op jit(solution)/shard_map/all_to_all | solution.py:293
  1673.8 13.6 fusion.107
  1687.4 38.0 %all-reduce.3 = (f32[2048]{0:T(1024)S(1)}, f32[2048]{0:T(1024)S(1)}) all-reduce(f32[2048]{0:T(1024)S(1)} %get-tuple-element.610, f32[2048]{0:T(1024)S(1)} %copy-done.22), channel_id=4, replica_groups=mesh['fsdp'=4,'seq'=8] {'fsdp','seq'}, use_global_device_ids=true, to_apply=%region_15.16.clone | all-reduce | flops 4096 | bytes 32768
  1737.1 77.2 %reduce-scatter.6.cloned.1.call-done = bf16[256,2,2048]{0,2,1:T(8,128)(2,1)} async-done(((bf16[1024,2,2048]{0,2,1:T(8,128)(2,1)}), bf16[256,2,2048]{0,2,1:T(8,128)(2,1)}) %reduce-scatter.6.cloned.1.call-update) | async-done | bytes 2097168 | tf_op jit(solution)/shard_map/reduce_scatter | solution.py:249
  1814.3 6.4 copy.222
  (280 shorter events, 152.2 us)
Async XLA Ops:
  7.2 233.0 %all-gather.11.cloned.1.call-start = ((), (), s32[]{:S(2)}) async-start(), calls=%async_computation.8 | async-start | bytes 31457280 | tf_op jit(solution)/shard_map/all_gather | solution.py:192
  7.9 387.4 %all-gather.13.cloned.1.call-start = ((), (), s32[]{:S(2)}) async-start(), calls=%async_computation.9 | async-start | bytes 10485760 | tf_op jit(solution)/shard_map/all_gather | solution.py:193
  8.7 899.4 %all-gather.15.cloned.1.call-start = ((), (), s32[]{:S(2)}) async-start(), calls=%async_computation.10 | async-start | bytes 83886080 | tf_op jit(solution)/shard_map/all_gather | solution.py:210
  26.8 1180.0 %all-gather.17.cloned.1.call-start = ((), (), s32[]{:S(2)}) async-start(), calls=%async_computation.11 | async-start | bytes 41943040 | tf_op jit(solution)/shard_map/all_gather | solution.py:211
  27.5 347.3 %copy-start.20 = (f32[2048]{0:T(1024)}, f32[2048]{0:T(1024)S(1)}, u32[]{:S(2)}) copy-start(f32[2048]{0:T(1024)S(1)} %convert_element_type.204) | copy-start | bytes 24580
  28.7 346.2 %copy-start.23 = (f32[128]{0:T(128)}, f32[128]{0:T(128)S(1)}, u32[]{:S(2)}) copy-start(f32[128]{0:T(128)S(1)} %get-tuple-element.712) | copy-start | bytes 1540
  270.8 5.3 copy-start.19
  278.9 54.1 %all-to-all-start = ((bf16[3,1,128,2048]{2,0,1,3:T(4,128)(2,1)}), bf16[3,1,128,2048]{2,0,1,3:T(4,128)(2,1)S(1)}, u32[]{:S(2)}, u32[]{:S(2)}) async-start(bf16[3,1,128,2048]{2,0,1,3:T(4,128)(2,1)} %copy.196), calls=%async_computation | async-start | bytes 4194304 | tf_op jit(solution)/shard_map/all_to_all | solution.py:200
  336.2 3.2 copy-start.14
  357.6 18.3 %copy-start.7 = (f32[1,1024,4,64]{1,3,2,0:T(8,128)}, f32[1,1024,4,64]{1,3,2,0:T(8,128)S(1)}, u32[]{:S(2)}) copy-start(f32[1,1024,4,64]{1,3,2,0:T(8,128)S(1)} %get-tuple-element.501) | copy-start | bytes 3145732
  357.6 17.3 copy-start.2
  357.6 18.5 %copy-start.26 = (bf16[2048]{0:T(1024)(128)(2,1)S(1)}, bf16[2048]{0:T(1024)(128)(2,1)}, u32[]{:S(2)}) copy-start(bf16[2048]{0:T(1024)(128)(2,1)} %param.18) | copy-start | bytes 12292
  370.7 19.5 %all-to-all-start.1 = ((bf16[8,2,16384]{2,1,0:T(2,128)(2,1)}), bf16[8,2,16384]{2,1,0:T(2,128)(2,1)}, u32[]{:S(2)}, u32[]{:S(2)}) async-start(bf16[8,2,16384]{2,1,0:T(2,128)(2,1)} %reshape.879), calls=%async_computation.1 | async-start | bytes 1048576 | tf_op jit(solution)/shard_map/all_to_all | solution.py:203
  374.8 1015.3 %all-gather.19.cloned.1.call-start = ((), (), s32[]{:S(2)}) async-start(), calls=%async_computation.12 | async-start | bytes 4718592 | tf_op jit(solution)/shard_map/all_gather | solution.py:271
  375.9 1029.6 %all-gather.23.cloned.1.call-start = ((), (), s32[]{:S(2)}) async-start(), calls=%async_computation.17 | async-start | bytes 4718592 | tf_op jit(solution)/shard_map/all_gather | solution.py:274
  401.8 849.5 %copy-start.4 = (f32[128,2048]{1,0:T(8,128)}, f32[128,2048]{1,0:T(8,128)S(1)}, u32[]{:S(2)}) copy-start(f32[128,2048]{1,0:T(8,128)S(1)} %get-tuple-element.716) | copy-start | bytes 3145732
  402.0 543.7 %copy-start.11 = (bf16[128,2048]{1,0:T(8,128)(2,1)}, bf16[128,2048]{1,0:T(8,128)(2,1)S(1)}, u32[]{:S(2)}) copy-start(bf16[128,2048]{1,0:T(8,128)(2,1)S(1)} %multiply_convert_fusion.2) | copy-start | bytes 1572868
  1226.0 25.4 %copy-start.16 = (bf16[1,128,2048]{2,1,0:T(8,128)(2,1)S(1)}, bf16[1,128,2048]{2,1,0:T(8,128)(2,1)}, u32[]{:S(2)}) copy-start(bf16[1,128,2048]{2,1,0:T(8,128)(2,1)} %param.23) | copy-start | bytes 1572868
  1252.9 324.7 %all-gather.21.cloned.1.call-start = ((), (), s32[]{:S(2)}) async-start(), calls=%async_computation.15 | async-start | bytes 4718592 | tf_op jit(solution)/shard_map/all_gather | solution.py:240
  1253.6 344.4 %all-gather.25.cloned.1.call-start = ((), (), s32[]{:S(2)}) async-start(), calls=%async_computation.18 | async-start | bytes 4718592 | tf_op jit(solution)/shard_map/all_gather | solution.py:237
  1254.4 6.0 copy-start.9
  1278.4 32.9 %all-to-all-start.2 = ((bf16[8,2,16384]{2,1,0:T(2,128)(2,1)}), bf16[8,2,16384]{2,1,0:T(2,128)(2,1)S(1)}, u32[]{:S(2)}, u32[]{:S(2)}) async-start(bf16[8,2,16384]{2,1,0:T(2,128)(2,1)} %reshape.881), calls=%async_computation.2 | async-start | bytes 1048576 | tf_op jit(solution)/shard_map/all_to_all | solution.py:267
  1311.3 256.2 %all-to-all-start.4 = ((bf16[3,1,128,8192]{2,0,1,3:T(4,128)(2,1)}), bf16[3,1,128,8192]{2,0,1,3:T(4,128)(2,1)}, u32[]{:S(2)}, u32[]{:S(2)}) async-start(bf16[3,1,128,8192]{2,0,1,3:T(4,128)(2,1)} %copy.216), calls=%async_computation.5 | async-start | bytes 16777216 | tf_op jit(solution)/shard_map/all_to_all | solution.py:236
  1316.2 8.6 copy-start.8
  1316.3 413.0 %all-reduce.6.cloned.1.call-start = ((), (), s32[]{:S(2)}) async-start(), calls=%async_computation.19 | async-start | bytes 8388608
  1331.7 2.7 copy-start.10
  1337.0 2.7 copy-start.10
  1345.0 2.7 copy-start.10
  1350.3 2.7 copy-start.10
  1355.7 2.7 copy-start.10
  1361.0 2.7 copy-start.10
  1372.7 4.6 copy-start.6
  1378.7 6.3 copy-start.13
  1390.1 7.6 copy-start.17
  1397.7 7.9 copy-start.15
  1405.5 327.3 %reduce-scatter.4.cloned.1.call-start = ((), (), s32[]{:S(2)}) async-start(), calls=%async_computation.13 | async-start | bytes 1310720 | tf_op jit(solution)/shard_map/reduce_scatter | solution.py:289
  1410.0 324.5 %reduce-scatter.8.cloned.1.call-start = ((), (), s32[]{:S(2)}) async-start(), calls=%async_computation.16 | async-start | bytes 5242880 | tf_op jit(solution)/shard_map/reduce_scatter | solution.py:252
  1572.1 2.7 copy-start
  1587.1 227.2 %reduce-scatter.6.cloned.1.call-start = ((), (), s32[]{:S(2)}) async-start(), calls=%async_computation.14 | async-start | bytes 10485760 | tf_op jit(solution)/shard_map/reduce_scatter | solution.py:249
  1613.5 6.5 copy-start.28
  1613.5 7.8 copy-start.5
  1616.2 52.8 %all-to-all-start.3 = ((bf16[3,1,1024,256]{3,0,1,2:T(4,128)(2,1)}), bf16[3,1,1024,256]{3,0,1,2:T(4,128)(2,1)S(1)}, u32[]{:S(2)}, u32[]{:S(2)}) async-start(bf16[3,1,1024,256]{3,0,1,2:T(4,128)(2,1)} %copy.210), calls=%async_computation.3 | async-start | bytes 4194304 | tf_op jit(solution)/shard_map/all_to_all | solution.py:293
  1640.2 33.6 %copy-start.3 = (bf16[1,128,2048]{2,1,0:T(8,128)(2,1)S(1)}, bf16[1,128,2048]{2,1,0:T(8,128)(2,1)}, u32[]{:S(2)}) copy-start(bf16[1,128,2048]{2,1,0:T(8,128)(2,1)} %param.16) | copy-start | bytes 1572868
  1640.2 33.6 %copy-start.21 = (f32[2048]{0:T(1024)S(1)}, f32[2048]{0:T(1024)}, u32[]{:S(2)}) copy-start(f32[2048]{0:T(1024)} %copy-done.20) | copy-start | bytes 24580
  1640.2 33.6 %copy-start.24 = (f32[128]{0:T(128)S(1)}, f32[128]{0:T(128)}, u32[]{:S(2)}) copy-start(f32[128]{0:T(128)} %copy-done.23) | copy-start | bytes 1540
  1673.8 13.6 copy-start.22
  1673.8 52.8 %copy-start.12 = (f32[128,2048]{1,0:T(8,128)S(1)}, f32[128,2048]{1,0:T(8,128)}, u32[]{:S(2)}) copy-start(f32[128,2048]{1,0:T(8,128)} %get-tuple-element.683) | copy-start | bytes 3145732
  1673.8 52.8 %copy-start.27 = (f32[128]{0:T(128)S(1)}, f32[128]{0:T(128)}, u32[]{:S(2)}) copy-start(f32[128]{0:T(128)} %get-tuple-element.711) | copy-start | bytes 1540
  (3 other events, 2.9 us)
Sparse Core Ops, SparseCore 0:
  9.8 230.2 all-gather.10
  242.0 87.4 all-gather.12
  331.4 576.6 all-gather.14
  909.8 297.0 all-gather.16
  1208.3 46.8 all-gather.18
  1257.3 56.8 all-gather.22
  1315.8 78.7 all-gather.20
  1396.2 135.9 all-gather.24
  1536.0 101.4 all-reduce.5
  1640.3 27.9 reduce-scatter.3
  1671.2 53.6 reduce-scatter.7
  1727.8 86.4 reduce-scatter.5
where the time goes:
time: 1840 us; the launch traced here: 1830 us
  waiting for transfers between devices  1320 us (72%)
  matrix products  220 us (12%)
  local copies, waits for them, and re-layouts  140 us (8%)
  other arithmetic  72.3 us (4%)
  blocking collectives  38 us (2%)
  starting transfers between devices  23.7 us (1%)
    all_gather x1, waiting for transfers between devices, body(): lax.all_gather(w_gate_up, 'fsdp', axis=0, tiled=True)  506 us
    all_gather x1, waiting for transfers between devices, body(): lax.all_gather(w_down, 'fsdp', axis=0, tiled=True)  261 us
    all_gather x1, waiting for transfers between devices, body(): lax.all_gather(w_qkv, 'fsdp', axis=0, tiled=True)  211 us
    all_to_all x1, waiting for transfers between devices, body(): lax.all_to_all(unit_rows, 'seq', split_axis=3, concat_axis=2, tiled=True)  157 us
    reduce_scatter x1, waiting for transfers between devices, body(): lax.psum_scatter(gu_part.astype(jnp.bfloat16), 'fsdp', scatter_dimension=...  77.2 us
    all_to_all x1, waiting for transfers between devices, body(): lax.all_to_all(stacked, 'seq', split_axis=3, concat_axis=2, tiled=True)  49 us
    unnamed x69, local copies, waits for them, and re-layouts  43.5 us
    unnamed x1, blocking collectives  38 us
  transfers between devices with their start and end apart: 17, of which 9 were waited for; matrix products, arithmetic and copies ran while one was open for 23% of the time, Pallas kernels for 0%

commit v1 on v0

--- a/solution.py
+++ b/solution.py
@@ -197,7 +197,10 @@
     key_rows = (projected[1] * cosine + rotate(projected[1]) * sine_table).astype(jnp.bfloat16)
     values = projected[2].astype(jnp.bfloat16)
     stacked = jnp.stack([queries, key_rows, values]).reshape(3, seq_count, shard_len, model_width)
-    head_view = lax.all_to_all(stacked, "seq", split_axis=3, concat_axis=2, tiled=True)
+    head_view = jnp.concatenate(
+        lax.all_to_all(jnp.stack(jnp.split(stacked, lax.axis_size("seq"), axis=3)), "seq", 0, 0),
+        axis=2,
+    )
     attended, totals = attend_forward(head_view[0], head_view[1], head_view[2])
     attended_heads = attended.astype(jnp.bfloat16)
     sent_back = lax.all_to_all(attended_heads, "seq", split_axis=1, concat_axis=2, tiled=True)

time: 1840 us -> 1840 us (level)
    unnamed x69 -> x74, local copies, waits for them, and re-layouts: 43.5 us -> 49.3 us
where the time goes in v1:
time: 1840 us; the launch traced here: 1830 us
  waiting for transfers between devices  1320 us (72%)
  matrix products  220 us (12%)
  local copies, waits for them, and re-layouts  139 us (8%)
  other arithmetic  72.3 us (4%)
  blocking collectives  38 us (2%)
  starting transfers between devices  23.7 us (1%)
    all_gather x1, waiting for transfers between devices, body(): lax.all_gather(w_gate_up, 'fsdp', axis=0, tiled=True)  520 us
    all_gather x1, waiting for transfers between devices, body(): lax.all_gather(w_down, 'fsdp', axis=0, tiled=True)  261 us
    all_gather x1, waiting for transfers between devices, body(): lax.all_gather(w_qkv, 'fsdp', axis=0, tiled=True)  211 us
    all_to_all x1, waiting for transfers between devices, body(): lax.all_to_all(unit_rows, 'seq', split_axis=3, concat_axis=2, tiled=True)  156 us
    reduce_scatter x1, waiting for transfers between devices, body(): lax.psum_scatter(gu_part.astype(jnp.bfloat16), 'fsdp', scatter_dimension=...  77.3 us
    unnamed x74, local copies, waits for them, and re-layouts  49.3 us
    unnamed x1, blocking collectives  38 us
    all_to_all x1, waiting for transfers between devices, body(): lax.all_to_all(jnp.stack(jnp.split(stacked, lax.axis_size('seq'), axis=3)...  37.8 us
  transfers between devices with their start and end apart: 17, of which 9 were waited for; matrix products, arithmetic and copies ran while one was open for 23% of the time, Pallas kernels for 0%

profile of v1, /device:TPU:0, one launch (start us, length us, event | category | flops | bytes accessed | tf_op | source)
XLA Modules:
  0.0 1827.8 jit_solution(17514729585084769290)
XLA Ops:
  8.7 18.1 copy.202
  28.7 211.5 %all-gather.11.cloned.1.call-done = bf16[2048,3,2048]{2,0,1:T(8,128)(2,1)} async-done(((bf16[512,3,2048]{2,0,1:T(8,128)(2,1)}), bf16[2048,3,2048]{2,0,1:T(8,128)(2,1)}) %all-gather.11.cloned.1.call-update) | async-done | bytes 25165840 | tf_op jit(solution)/shard_map/all_gather | solution.py:192
  240.2 13.5 convolution_bitcast_fusion.3
  270.9 5.3 fusion.111
  282.0 4.9 all-to-all-start
  286.9 37.8 %all-to-all-done = bf16[8,3,1,128,256]{4,3,1,2,0:T(8,128)(2,1)S(1)} async-done(((bf16[8,3,1,128,256]{4,3,1,2,0:T(8,128)(2,1)}), bf16[8,3,1,128,256]{4,3,1,2,0:T(8,128)(2,1)S(1)}, u32[]{:S(2)}, u32[]{:S(2)}) %all-to-all-start) | async-done | bytes 1572896 | tf_op jit(solution)/shard_map/all_to_all | solution.py:201
  326.6 16.6 while.118
  327.5 4.9 while.121
  333.3 9.9 while.121
  344.2 3.8 copy.200
  348.5 5.9 reduce.3
  356.4 4.2 all-to-all-start.1
  362.3 13.7 all-to-all-done.1
  381.1 6.5 multiply_reduce_fusion.3
  387.8 520.3 %all-gather.15.cloned.1.call-done = bf16[8192,2,2048]{2,0,1:T(8,128)(2,1)} async-done(((bf16[2048,2,2048]{2,0,1:T(8,128)(2,1)}), bf16[8192,2,2048]{2,0,1:T(8,128)(2,1)}) %all-gather.15.cloned.1.call-update) | async-done | bytes 67108880 | tf_op jit(solution)/shard_map/all_gather | solution.py:213
  908.1 37.6 %convolution_bitcast_fusion.2 = f32[2,128,8192]{2,1,0:T(8,128)} fusion(bf16[8192,2,2048]{2,0,1:T(8,128)(2,1)} %all-gather.15.cloned.1.call-done, bf16[128,2048]{1,0:T(8,128)(2,1)S(1)} %multiply_convert_fusion.2), kind=kOutput, calls=%fused_computation.67 | convolution fusion | flops 8589934592 | bytes 76021760 | tf_op jit(solution)/shard_map/td,jpd->ptj/dot_general | solution.py:216
  945.7 261.2 %all-gather.17.cloned.1.call-done = bf16[2048,8192]{1,0:T(8,128)(2,1)} async-done(((bf16[512,8192]{1,0:T(8,128)(2,1)}), bf16[2048,8192]{1,0:T(8,128)(2,1)}) %all-gather.17.cloned.1.call-update) | async-done | bytes 33554448 | tf_op jit(solution)/shard_map/all_gather | solution.py:214
  1206.9 19.1 %fusion.83 = (bf16[1,128,8192]{2,1,0:T(8,128)(2,1)}, bf16[1,128,8192]{2,1,0:T(8,128)(2,1)}) fusion(f32[2,128,8192]{2,1,0:T(8,128)} %convolution_bitcast_fusion.2, bf16[2048,8192]{1,0:T(8,128)(2,1)} %all-gather.17.cloned.1.call-done, bf16[1,128,2048]{2,1,0:T(8,128)(2,1)} %param.23), kind=kOutput, calls=%fused_computation.108 | convolution fusion | flops 4308598784 | bytes 46661632 | tf_op jit(solution)/shard_map/tf,fj->tj/dot_general | solution.py:227
  1226.0 25.4 %multiply_reduce_fusion = (f32[2048]{0:T(1024)}, f32[128]{0:T(128)S(1)}, f32[128,2048]{1,0:T(8,128)S(1)}) fusion(f32[128,2048]{1,0:T(8,128)S(1)} %get-tuple-element.731, f32[128]{0:T(128)S(1)} %get-tuple-element.729, f32[2048]{0:T(1024)S(1)} %convert_element_type.212, bf16[8192,2,2048]{2,0,1:T(8,128)(2,1)} %all-gather.15.cloned.1.call-done, ...), kind=kOutput, calls=%fused_computation.151 | convolution fusion | flops 8593602560 | bytes 73417728 | tf_op jit(solution)/shard_map/ptj,jpd->td/dot_general | solution.py:232
  1254.4 6.0 multiply_convert_fusion
  1260.3 4.9 fusion.79
  1266.0 11.5 reduce.4
  1278.5 4.5 all-to-all-start.2
  1282.9 6.5 maximum_bitcast_fusion
  1289.4 13.2 copy.216
  1302.6 8.7 all-to-all-done.2
  1311.3 4.9 all-to-all-start.4
  1329.2 37.6 %while.120 = (s32[]{:T(128)}, f32[1,1024,4,64]{1,3,2,0:T(8,128)}, f32[1,1024,4,64]{1,3,2,0:T(8,128)S(1)}, f32[1,1024,4,64]{1,3,2,0:T(8,128)}, bf16[1,1024,4,64]{...) while((s32[]{:T(128)}, f32[1,1024,4,64]{1,3,2,0:T(8,128)}, ...), condition=%wide.region_12.13_spmd, body=%wide.region_9.12_spmd.sunk | while | flops 340329248 | bytes 17070880 | solution.py:170
  1331.0 10.8 while.122
  1344.4 21.6 %while.122 = (s32[]{:T(128)}, f32[1,512,4,64]{1,3,2,0:T(8,128)S(1)}, f32[1,1024,4,64]{1,3,2,0:T(8,128)S(1)}, f32[1,1024,4,64]{1,3,2,0:T(8,128)}, s32[]{:T(128)},...) while((s32[]{:T(128)}, f32[1,512,4,64]{1,3,2,0:T(8,128)S(1)}, ...), condition=%wide.region_11.11_spmd.clone, body=%wide.region_10.10_spmd.clone.sunk | while | flops 340329216 | bytes 14432507 | solution.py:163
  1368.1 4.8 fusion.115
  1385.1 5.2 add_convert_fusion.1
  1390.3 7.5 fusion.72
  1397.9 8.1 copy.215
  1407.0 4.4 convolution_convert_fusion
  1411.4 156.1 %all-to-all-done.4 = bf16[3,1,128,8192]{2,0,1,3:T(4,128)(2,1)} async-done(((bf16[3,1,128,8192]{2,0,1,3:T(4,128)(2,1)}), bf16[3,1,128,8192]{2,0,1,3:T(4,128)(2,1)}, u32[]{:S(2)}, u32[]{:S(2)}) %all-to-all-start.4) | async-done | bytes 6291488 | tf_op jit(solution)/shard_map/all_to_all | solution.py:239
  1567.5 4.6 copy.217
  1577.5 9.5 convert_bitcast_fusion.1
  1587.1 4.6 slice.103
  1591.7 6.3 copy.218
  1598.0 14.1 convert_bitcast_fusion
  1616.1 3.8 all-to-all-start.3
  1621.2 19.0 %fusion.80 = bf16[1,128,2048]{2,1,0:T(8,128)(2,1)} fusion(f32[128,2048]{1,0:T(8,128)S(1)} %copy-done.5, bf16[2048,8192]{1,0:T(8,128)(2,1)} %all-gather.17.cloned.1.call-done, f32[2,128,8192]{2,1,0:T(8,128)} %convolution_bitcast_fusion.2), kind=kOutput, calls=%fused_computation.106 | convolution fusion | flops 4301783040 | bytes 43515904 | tf_op jit(solution)/shard_map/tj,fj->tf/dot_general | solution.py:218
  1640.2 28.7 %all-to-all-done.3 = bf16[3,1,1024,256]{3,0,1,2:T(4,128)(2,1)S(1)} async-done(((bf16[3,1,1024,256]{3,0,1,2:T(4,128)(2,1)}), bf16[3,1,1024,256]{3,0,1,2:T(4,128)(2,1)S(1)}, u32[]{:S(2)}, u32[]{:S(2)}) %all-to-all-start.3) | async-done | bytes 1572896 | tf_op jit(solution)/shard_map/all_to_all | solution.py:296
  1673.8 13.6 fusion.107
  1687.4 38.0 %all-reduce.3 = (f32[2048]{0:T(1024)S(1)}, f32[2048]{0:T(1024)S(1)}) all-reduce(f32[2048]{0:T(1024)S(1)} %get-tuple-element.625, f32[2048]{0:T(1024)S(1)} %copy-done.21), channel_id=4, replica_groups=mesh['fsdp'=4,'seq'=8] {'fsdp','seq'}, use_global_device_ids=true, to_apply=%region_15.16.clone | all-reduce | flops 4096 | bytes 32768
  1737.1 77.3 %reduce-scatter.6.cloned.1.call-done = bf16[256,2,2048]{0,2,1:T(8,128)(2,1)} async-done(((bf16[1024,2,2048]{0,2,1:T(8,128)(2,1)}), bf16[256,2,2048]{0,2,1:T(8,128)(2,1)}) %reduce-scatter.6.cloned.1.call-update) | async-done | bytes 2097168 | tf_op jit(solution)/shard_map/reduce_scatter | solution.py:252
  1814.4 6.4 copy.222
  (285 shorter events, 150.6 us)
Async XLA Ops:
  7.2 233.0 %all-gather.11.cloned.1.call-start = ((), (), s32[]{:S(2)}) async-start(), calls=%async_computation.8 | async-start | bytes 31457280 | tf_op jit(solution)/shard_map/all_gather | solution.py:192
  7.9 373.2 %all-gather.13.cloned.1.call-start = ((), (), s32[]{:S(2)}) async-start(), calls=%async_computation.9 | async-start | bytes 10485760 | tf_op jit(solution)/shard_map/all_gather | solution.py:193
  8.7 899.4 %all-gather.15.cloned.1.call-start = ((), (), s32[]{:S(2)}) async-start(), calls=%async_computation.10 | async-start | bytes 83886080 | tf_op jit(solution)/shard_map/all_gather | solution.py:213
  26.8 1.1 copy-start.1
  26.9 1180.0 %all-gather.17.cloned.1.call-start = ((), (), s32[]{:S(2)}) async-start(), calls=%async_computation.11 | async-start | bytes 41943040 | tf_op jit(solution)/shard_map/all_gather | solution.py:214
  27.5 333.1 %copy-start.19 = (f32[2048]{0:T(1024)}, f32[2048]{0:T(1024)S(1)}, u32[]{:S(2)}) copy-start(f32[2048]{0:T(1024)S(1)} %convert_element_type.204) | copy-start | bytes 24580
  28.7 332.0 %copy-start.22 = (f32[128]{0:T(128)}, f32[128]{0:T(128)S(1)}, u32[]{:S(2)}) copy-start(f32[128]{0:T(128)S(1)} %get-tuple-element.727) | copy-start | bytes 1540
  270.9 5.3 copy-start.18
  282.0 42.7 %all-to-all-start = ((bf16[8,3,1,128,256]{4,3,1,2,0:T(8,128)(2,1)}), bf16[8,3,1,128,256]{4,3,1,2,0:T(8,128)(2,1)S(1)}, u32[]{:S(2)}, u32[]{:S(2)}) async-start(bf16[8,3,1,128,256]{4,3,1,2,0:T(8,128)(2,1)} %fusion.123), calls=%async_computation | async-start | bytes 3145728 | tf_op jit(solution)/shard_map/all_to_all | solution.py:201
  343.3 13.2 copy-start.7
  343.3 17.4 copy-start.2
  344.2 18.1 copy-start.25
  356.4 19.5 %all-to-all-start.1 = ((bf16[8,2,16384]{2,1,0:T(2,128)(2,1)}), bf16[8,2,16384]{2,1,0:T(2,128)(2,1)}, u32[]{:S(2)}, u32[]{:S(2)}) async-start(bf16[8,2,16384]{2,1,0:T(2,128)(2,1)} %reshape.884), calls=%async_computation.1 | async-start | bytes 1048576 | tf_op jit(solution)/shard_map/all_to_all | solution.py:206
  360.6 1029.7 %all-gather.19.cloned.1.call-start = ((), (), s32[]{:S(2)}) async-start(), calls=%async_computation.12 | async-start | bytes 4718592 | tf_op jit(solution)/shard_map/all_gather | solution.py:274
  361.7 1044.3 %all-gather.23.cloned.1.call-start = ((), (), s32[]{:S(2)}) async-start(), calls=%async_computation.17 | async-start | bytes 4718592 | tf_op jit(solution)/shard_map/all_gather | solution.py:277
  387.6 863.7 %copy-start.4 = (f32[128,2048]{1,0:T(8,128)}, f32[128,2048]{1,0:T(8,128)S(1)}, u32[]{:S(2)}) copy-start(f32[128,2048]{1,0:T(8,128)S(1)} %get-tuple-element.731) | copy-start | bytes 3145732
  387.8 557.9 %copy-start.11 = (bf16[128,2048]{1,0:T(8,128)(2,1)}, bf16[128,2048]{1,0:T(8,128)(2,1)S(1)}, u32[]{:S(2)}) copy-start(bf16[128,2048]{1,0:T(8,128)(2,1)S(1)} %multiply_convert_fusion.2) | copy-start | bytes 1572868
  1226.0 25.4 %copy-start.15 = (bf16[1,128,2048]{2,1,0:T(8,128)(2,1)S(1)}, bf16[1,128,2048]{2,1,0:T(8,128)(2,1)}, u32[]{:S(2)}) copy-start(bf16[1,128,2048]{2,1,0:T(8,128)(2,1)} %param.23) | copy-start | bytes 1572868
  1252.9 324.7 %all-gather.21.cloned.1.call-start = ((), (), s32[]{:S(2)}) async-start(), calls=%async_computation.15 | async-start | bytes 4718592 | tf_op jit(solution)/shard_map/all_gather | solution.py:243
  1253.6 344.4 %all-gather.25.cloned.1.call-start = ((), (), s32[]{:S(2)}) async-start(), calls=%async_computation.18 | async-start | bytes 4718592 | tf_op jit(solution)/shard_map/all_gather | solution.py:240
  1254.4 6.0 copy-start.9
  1278.5 32.9 %all-to-all-start.2 = ((bf16[8,2,16384]{2,1,0:T(2,128)(2,1)}), bf16[8,2,16384]{2,1,0:T(2,128)(2,1)S(1)}, u32[]{:S(2)}, u32[]{:S(2)}) async-start(bf16[8,2,16384]{2,1,0:T(2,128)(2,1)} %reshape.886), calls=%async_computation.2 | async-start | bytes 1048576 | tf_op jit(solution)/shard_map/all_to_all | solution.py:270
  1311.3 256.2 %all-to-all-start.4 = ((bf16[3,1,128,8192]{2,0,1,3:T(4,128)(2,1)}), bf16[3,1,128,8192]{2,0,1,3:T(4,128)(2,1)}, u32[]{:S(2)}, u32[]{:S(2)}) async-start(bf16[3,1,128,8192]{2,0,1,3:T(4,128)(2,1)} %copy.216), calls=%async_computation.5 | async-start | bytes 16777216 | tf_op jit(solution)/shard_map/all_to_all | solution.py:239
  1316.3 412.9 %all-reduce.6.cloned.1.call-start = ((), (), s32[]{:S(2)}) async-start(), calls=%async_computation.19 | async-start | bytes 8388608
  1318.3 6.3 copy-start.8
  1331.7 2.6 copy-start.10
  1337.1 2.6 copy-start.10
  1345.1 2.6 copy-start.10
  1350.5 2.6 copy-start.10
  1355.9 2.6 copy-start.10
  1361.3 2.6 copy-start.10
  1373.9 3.6 copy-start.6
  1380.9 4.2 copy-start.13
  1390.3 7.6 copy-start.16
  1405.9 326.7 %reduce-scatter.4.cloned.1.call-start = ((), (), s32[]{:S(2)}) async-start(), calls=%async_computation.13 | async-start | bytes 1310720 | tf_op jit(solution)/shard_map/reduce_scatter | solution.py:292
  1411.4 323.1 %reduce-scatter.8.cloned.1.call-start = ((), (), s32[]{:S(2)}) async-start(), calls=%async_computation.16 | async-start | bytes 5242880 | tf_op jit(solution)/shard_map/reduce_scatter | solution.py:255
  1572.1 2.7 copy-start
  1587.1 227.3 %reduce-scatter.6.cloned.1.call-start = ((), (), s32[]{:S(2)}) async-start(), calls=%async_computation.14 | async-start | bytes 10485760 | tf_op jit(solution)/shard_map/reduce_scatter | solution.py:252
  1612.1 1.1 copy-start.17
  1613.4 6.5 copy-start.27
  1613.4 7.7 copy-start.5
  1616.1 52.7 %all-to-all-start.3 = ((bf16[3,1,1024,256]{3,0,1,2:T(4,128)(2,1)}), bf16[3,1,1024,256]{3,0,1,2:T(4,128)(2,1)S(1)}, u32[]{:S(2)}, u32[]{:S(2)}) async-start(bf16[3,1,1024,256]{3,0,1,2:T(4,128)(2,1)} %copy.210), calls=%async_computation.3 | async-start | bytes 4194304 | tf_op jit(solution)/shard_map/all_to_all | solution.py:296
  1669.1 4.7 copy-start.3
  1669.1 4.7 copy-start.20
  1669.1 4.7 copy-start.23
  1673.8 13.6 copy-start.21
  1673.8 52.7 %copy-start.12 = (f32[128,2048]{1,0:T(8,128)S(1)}, f32[128,2048]{1,0:T(8,128)}, u32[]{:S(2)}) copy-start(f32[128,2048]{1,0:T(8,128)} %get-tuple-element.698) | copy-start | bytes 3145732
  1673.8 52.7 %copy-start.26 = (f32[128]{0:T(128)S(1)}, f32[128]{0:T(128)}, u32[]{:S(2)}) copy-start(f32[128]{0:T(128)} %get-tuple-element.726) | copy-start | bytes 1540
  (2 other events, 1.7 us)
Sparse Core Ops, SparseCore 0:
  9.8 230.2 all-gather.10
  242.0 87.4 all-gather.12
  331.4 576.6 all-gather.14
  909.8 297.0 all-gather.16
  1208.3 46.8 all-gather.18
  1257.3 56.8 all-gather.22
  1315.8 78.7 all-gather.20
  1396.2 135.9 all-gather.24
  1536.1 101.4 all-reduce.5
  1640.3 27.9 reduce-scatter.3
  1671.2 53.6 reduce-scatter.7
  1727.9 86.4 reduce-scatter.5
